TPU v7x, 32 devices: a whole 2x2x4 slice. The times are simulated.
32 devices in a mesh: narrow: 2 (over y), wide: 16 (over z, x, core).
Axes of the slice: x: 2, y: 2, z: 4, core: 2. Of those that a mesh axis runs over, the one named last changes fastest.
Arguments:
- layer_input: bfloat16 [2, 2048, 2048], P('narrow', 'wide'), may hold values from -6 to 6
- lengths: int32 [2], P('narrow'), may hold values from 768 to 2048, as said below
- attn_gain: bfloat16 [2048], replicated, may hold values from 0.5 to 1.5
- w_query: bfloat16 [2048, 2048], P('wide'), may hold values from -0.125 to 0.125
- w_key: bfloat16 [2048, 2048], P('wide'), may hold values from -0.125 to 0.125
- w_value: bfloat16 [2048, 2048], P('wide'), may hold values from -0.125 to 0.125
- w_out: bfloat16 [2048, 2048], P('wide'), may hold values from -3 to 3
- mlp_gain: bfloat16 [2048], replicated, may hold values from 0.5 to 1.5
- w_gate: bfloat16 [8192, 2048], P('wide'), may hold values from -0.125 to 0.125
- w_up: bfloat16 [8192, 2048], P('wide'), may hold values from -0.125 to 0.125
- w_down: bfloat16 [8192, 2048], P('wide'), may hold values from -0.0625 to 0.0625
- cotangent: bfloat16 [2, 2048, 2048], P('narrow', 'wide'), may hold values from -8 to 8
Outputs:
- block_output: bfloat16 [2, 2048, 2048], P('narrow', 'wide')
- input_grad: float32 [2, 2048, 2048], P('narrow', 'wide')
- grad_attn_gain: float32 [2048], replicated
- grad_query: float32 [2048, 2048], P('wide')
- grad_key: float32 [2048, 2048], P('wide')
- grad_value: float32 [2048, 2048], P('wide')
- grad_out: float32 [2048, 2048], P('wide')
- grad_mlp_gain: float32 [2048], replicated
- grad_gate: float32 [8192, 2048], P('wide')
- grad_up: float32 [8192, 2048], P('wide')
- grad_down: float32 [8192, 2048], P('wide')
Inputs may be any that keep to these rules, and one draw needn't show every extreme that they name: `lengths`: valid positions of each sequence, counted from its start; in every draw one sequence fills all 2048 positions.
All inputs are finite; a program needn't handle non-finite values.
Results may differ from a plain program's by a relative error of at most 0.017.
Values may be sent and summed in bfloat16 or wider, within the bound.
No kernel may reach another device: no remote copies, remote signals or barrier semaphores. Data moves between devices by JAX's collectives and lax.ppermute only.
A program may use at most 768 MiB of HBM per device.

v0:
```python
import math
import jax
import jax.numpy as jnp
from jax import lax
from jax.sharding import PartitionSpec as P

HEAD_DIM = 64
EPSILON = 1e-05
THETA = 130000.0
NEGATIVE = -1e30


def contract_rows(left_side, right_side):
    return lax.dot_general(
        left_side, right_side, (((0,), (0,)), ((), ())), preferred_element_type=jnp.float32
    )


def contract_cols(left_side, right_side):
    return lax.dot_general(
        left_side, right_side, (((1,), (1,)), ((), ())), preferred_element_type=jnp.float32
    )


def split_heads(matrix):
    return matrix.reshape(matrix.shape[0], -1, HEAD_DIM)


def rotate(tensor):
    half_dim = tensor.shape[-1] // 2
    return jnp.concatenate([-tensor[..., half_dim:], tensor[..., :half_dim]], axis=-1)


def rotary_tables(positions):
    half_dim = HEAD_DIM // 2
    frequency = THETA ** (-jnp.arange(half_dim, dtype=jnp.float32) * 2.0 / HEAD_DIM)
    angles = positions.astype(jnp.float32)[:, None] * frequency[None, :]
    cosine_table = jnp.concatenate([jnp.cos(angles), jnp.cos(angles)], axis=-1)[:, None, :]
    sine_table = jnp.concatenate([jnp.sin(angles), jnp.sin(angles)], axis=-1)[:, None, :]
    return (cosine_table, sine_table)


def rms_factor(matrix):
    return lax.rsqrt(jnp.mean(matrix * matrix, axis=-1, keepdims=True) + EPSILON)


def norm_back(upstream, normed, gain_vec, factor):
    scaled = upstream * gain_vec
    return factor * (scaled - normed * jnp.mean(scaled * normed, axis=-1, keepdims=True))


def swiglu_back(hidden_back, gate_proj, up_proj):
    sigmoid_gate = jax.nn.sigmoid(gate_proj)
    gate_back = (
        hidden_back * up_proj * sigmoid_gate * (1.0 + gate_proj * (1.0 - sigmoid_gate))
    ).astype(jnp.bfloat16)
    up_back = (hidden_back * jax.nn.silu(gate_proj)).astype(jnp.bfloat16)
    return (gate_back, up_back)


def over_blocks(carried, arrays, needed, work):
    row_total = arrays[0].shape[0]
    block_size = math.gcd(row_total, 512)
    block_count = row_total // block_size
    stacked = tuple(
        (member.reshape((block_count, block_size) + member.shape[1:]) for member in arrays)
    )

    def advance(state_now, scan_item):
        block_start = scan_item[0] * block_size

        def run_block(state_in):
            return work(state_in, scan_item[1:], block_start)

        def keep_block(state_in):
            return state_in

        return (lax.cond(needed(block_start, block_size), run_block, keep_block, state_now), None)

    finished, unused = lax.scan(
        advance, carried, (jnp.arange(block_count, dtype=jnp.int32),) + stacked
    )
    return finished


def shards(
    layer_input,
    lengths,
    attn_gain,
    w_query,
    w_key,
    w_value,
    w_out,
    mlp_gain,
    w_gate,
    w_up,
    w_down,
    cotangent,
):
    local_rows = layer_input.shape[1]
    model_width = layer_input.shape[2]
    head_count = model_width // HEAD_DIM
    score_scale = HEAD_DIM ** (-0.5)
    length = lengths[0]
    first_pos = lax.axis_index("wide") * local_rows
    last_pos = first_pos + local_rows - 1
    positions = first_pos + jnp.arange(local_rows, dtype=jnp.int32)
    valid_rows = (positions < length).astype(jnp.float32)[:, None]
    cosine_table, sine_table = rotary_tables(positions)
    inputs = layer_input[0].astype(jnp.float32)
    gain_one = attn_gain.astype(jnp.float32)
    gain_two = mlp_gain.astype(jnp.float32)
    full_query, full_key, full_value, full_out = (
        lax.all_gather(w_query, "wide", axis=0, tiled=True),
        lax.all_gather(w_key, "wide", axis=0, tiled=True),
        lax.all_gather(w_value, "wide", axis=0, tiled=True),
        lax.all_gather(w_out, "wide", axis=0, tiled=True),
    )
    factor_one = rms_factor(inputs)
    normed_one = inputs * factor_one
    norm_one = (normed_one * gain_one).astype(jnp.bfloat16)
    query_lin = split_heads(jnp.dot(norm_one, full_query, preferred_element_type=jnp.float32))
    key_lin = split_heads(jnp.dot(norm_one, full_key, preferred_element_type=jnp.float32))
    query_rot = (query_lin * cosine_table + rotate(query_lin) * sine_table).astype(jnp.bfloat16)
    key_rot = (key_lin * cosine_table + rotate(key_lin) * sine_table).astype(jnp.bfloat16)
    value_heads = split_heads(
        jnp.dot(norm_one, full_value, preferred_element_type=jnp.float32)
    ).astype(jnp.bfloat16)
    key_flat = key_rot.reshape(local_rows, model_width)
    value_flat = value_heads.reshape(local_rows, model_width)

    def keys_needed(block_start, block_size):
        return (block_start <= last_pos) & (block_start < length)

    def queries_needed(block_start, block_size):
        return (block_start + block_size - 1 >= first_pos) & (first_pos < length)

    def key_mask(block_start, block_size):
        key_pos = block_start + jnp.arange(block_size, dtype=jnp.int32)
        return ((key_pos[None, :] <= positions[:, None]) & (key_pos[None, :] < length))[None]

    def forward_block(state_in, blocks, block_start):
        row_best, denominator, accumulated = state_in
        block_keys = split_heads(blocks[0])
        block_values = split_heads(blocks[1])
        allowed = key_mask(block_start, block_keys.shape[0])
        scores = (
            jnp.einsum("qhd,khd->hqk", query_rot, block_keys, preferred_element_type=jnp.float32)
            * score_scale
        )
        scores = jnp.where(allowed, scores, NEGATIVE)
        new_best = jnp.maximum(row_best, jnp.max(scores, axis=-1))
        weights_exp = jnp.where(allowed, jnp.exp(scores - new_best[:, :, None]), 0.0)
        shrink = jnp.exp(row_best - new_best)
        denominator = denominator * shrink + jnp.sum(weights_exp, axis=-1)
        update = jnp.einsum(
            "hqk,khd->qhd",
            weights_exp.astype(jnp.bfloat16),
            block_values,
            preferred_element_type=jnp.float32,
        )
        accumulated = accumulated * shrink.T[:, :, None] + update
        return (new_best, denominator, accumulated)

    forward_start = (
        jnp.full((head_count, local_rows), NEGATIVE, jnp.float32),
        jnp.zeros((head_count, local_rows), jnp.float32),
        jnp.zeros((local_rows, head_count, HEAD_DIM), jnp.float32),
    )
    row_best, denominator, accumulated = over_blocks(
        forward_start,
        (
            lax.all_gather(key_flat, "wide", axis=0, tiled=True),
            lax.all_gather(value_flat, "wide", axis=0, tiled=True),
        ),
        keys_needed,
        forward_block,
    )
    log_total = row_best + jnp.log(denominator)
    attention = (
        (accumulated / denominator.T[:, :, None])
        .reshape(local_rows, model_width)
        .astype(jnp.bfloat16)
    )
    residual = inputs + jnp.dot(attention, full_out, preferred_element_type=jnp.float32)
    factor_two = rms_factor(residual)
    normed_two = residual * factor_two
    norm_two = (normed_two * gain_two).astype(jnp.bfloat16)
    group_norm = lax.all_gather(norm_two, "wide", axis=0, tiled=True)
    gate_proj = contract_cols(group_norm, w_gate)
    up_proj = contract_cols(group_norm, w_up)
    hidden = (jax.nn.silu(gate_proj) * up_proj).astype(jnp.bfloat16)
    mlp_out = lax.psum_scatter(
        jnp.dot(hidden, w_down, preferred_element_type=jnp.float32),
        "wide",
        scatter_dimension=0,
        tiled=True,
    )
    block_output = (residual + mlp_out).astype(jnp.bfloat16)
    y_back = cotangent[0].astype(jnp.float32) * valid_rows
    mlp_back = y_back.astype(jnp.bfloat16)
    group_back = lax.all_gather(mlp_back, "wide", axis=0, tiled=True)
    hidden_back = contract_cols(group_back, w_down)
    gate_back, up_back = swiglu_back(hidden_back, gate_proj, up_proj)
    norm_two_back = lax.psum_scatter(
        jnp.dot(gate_back, w_gate, preferred_element_type=jnp.float32)
        + jnp.dot(up_back, w_up, preferred_element_type=jnp.float32),
        "wide",
        scatter_dimension=0,
        tiled=True,
    )
    gate_part = contract_rows(gate_back, group_norm)
    up_part = contract_rows(up_back, group_norm)
    down_part = contract_rows(hidden, group_back)
    residual_back = y_back + norm_back(norm_two_back, normed_two, gain_two, factor_two)
    gain_two_term = jnp.sum(norm_two_back * normed_two, axis=0)
    branch_back = residual_back.astype(jnp.bfloat16)
    attention_back = contract_cols(branch_back, full_out).astype(jnp.bfloat16)
    row_delta = jnp.sum(
        (attention_back.astype(jnp.float32) * attention.astype(jnp.float32)).reshape(
            local_rows, head_count, HEAD_DIM
        ),
        axis=-1,
    ).T
    back_heads = split_heads(attention_back)

    def query_grad_block(state_in, blocks, block_start):
        block_keys = split_heads(blocks[0])
        block_values = split_heads(blocks[1])
        allowed = key_mask(block_start, block_keys.shape[0])
        scores = (
            jnp.einsum("qhd,khd->hqk", query_rot, block_keys, preferred_element_type=jnp.float32)
            * score_scale
        )
        prob_block = jnp.where(allowed, jnp.exp(scores - log_total[:, :, None]), 0.0)
        pulled = jnp.einsum(
            "qhd,khd->hqk", back_heads, block_values, preferred_element_type=jnp.float32
        )
        score_back = (prob_block * (pulled - row_delta[:, :, None]) * score_scale).astype(
            jnp.bfloat16
        )
        return state_in + jnp.einsum(
            "hqk,khd->qhd", score_back, block_keys, preferred_element_type=jnp.float32
        )

    query_back = over_blocks(
        jnp.zeros((local_rows, head_count, HEAD_DIM), jnp.float32),
        (
            lax.all_gather(key_flat, "wide", axis=0, tiled=True),
            lax.all_gather(value_flat, "wide", axis=0, tiled=True),
        ),
        keys_needed,
        query_grad_block,
    )

    def key_grad_block(state_in, blocks, block_start):
        key_back, value_back = state_in
        block_query = split_heads(blocks[0].astype(jnp.bfloat16))
        block_back = split_heads(blocks[1].astype(jnp.bfloat16))
        block_size = block_query.shape[0]
        query_pos = block_start + jnp.arange(block_size, dtype=jnp.int32)
        allowed = ((positions[None, :] <= query_pos[:, None]) & (positions[None, :] < length))[None]
        scores = (
            jnp.einsum("qhd,khd->hqk", block_query, key_rot, preferred_element_type=jnp.float32)
            * score_scale
        )
        prob_block = jnp.where(allowed, jnp.exp(scores - blocks[2].T[:, :, None]), 0.0)
        value_back = value_back + jnp.einsum(
            "hqk,qhd->khd",
            prob_block.astype(jnp.bfloat16),
            block_back,
            preferred_element_type=jnp.float32,
        )
        pulled = jnp.einsum(
            "qhd,khd->hqk", block_back, value_heads, preferred_element_type=jnp.float32
        )
        score_back = (prob_block * (pulled - blocks[3].T[:, :, None]) * score_scale).astype(
            jnp.bfloat16
        )
        key_back = key_back + jnp.einsum(
            "hqk,qhd->khd", score_back, block_query, preferred_element_type=jnp.float32
        )
        return (key_back, value_back)

    query_wire = query_rot.reshape(local_rows, model_width).astype(jnp.float32)
    back_wire = attention_back.astype(jnp.float32)
    zero_heads = jnp.zeros((local_rows, head_count, HEAD_DIM), jnp.float32)
    key_back, value_back = over_blocks(
        (zero_heads, zero_heads),
        (
            lax.all_gather(query_wire, "wide", axis=0, tiled=True),
            lax.all_gather(back_wire, "wide", axis=0, tiled=True),
            lax.all_gather(log_total.T, "wide", axis=0, tiled=True),
            lax.all_gather(row_delta.T, "wide", axis=0, tiled=True),
        ),
        queries_needed,
        key_grad_block,
    )
    query_lin_back = (
        (query_back * cosine_table - rotate(query_back * sine_table))
        .reshape(local_rows, model_width)
        .astype(jnp.bfloat16)
    )
    key_lin_back = (
        (key_back * cosine_table - rotate(key_back * sine_table))
        .reshape(local_rows, model_width)
        .astype(jnp.bfloat16)
    )
    value_lin_back = value_back.reshape(local_rows, model_width).astype(jnp.bfloat16)
    norm_one_back = (
        contract_cols(query_lin_back, full_query)
        + contract_cols(key_lin_back, full_key)
        + contract_cols(value_lin_back, full_value)
    )
    input_back = residual_back + norm_back(norm_one_back, normed_one, gain_one, factor_one)
    gain_one_term = jnp.sum(norm_one_back * normed_one, axis=0)
    attention_part = lax.psum_scatter(
        jnp.concatenate(
            [
                contract_rows(norm_one, query_lin_back),
                contract_rows(norm_one, key_lin_back),
                contract_rows(norm_one, value_lin_back),
                contract_rows(attention, branch_back),
            ],
            axis=1,
        ),
        "wide",
        scatter_dimension=0,
        tiled=True,
    )
    gain_totals = lax.psum((gain_one_term, gain_two_term), ("narrow", "wide"))
    summed = lax.psum((attention_part, gate_part, up_part, down_part), "narrow")
    attention_sum = summed[0]
    return (
        block_output[None],
        input_back[None],
        gain_totals[0],
        attention_sum[:, :model_width],
        attention_sum[:, model_width : 2 * model_width],
        attention_sum[:, 2 * model_width : 3 * model_width],
        attention_sum[:, 3 * model_width :],
        gain_totals[1],
        summed[1],
        summed[2],
        summed[3],
    )


def solution(mesh):
    placed = (
        P("narrow", "wide", None),
        P("narrow"),
        P(),
        P("wide", None),
        P("wide", None),
        P("wide", None),
        P("wide", None),
        P(),
        P("wide", None),
        P("wide", None),
        P("wide", None),
        P("narrow", "wide", None),
    )
    return jax.shard_map(
        shards,
        mesh=mesh,
        in_specs=placed,
        out_specs=(
            P("narrow", "wide", None),
            P("narrow", "wide", None),
            P(),
            P("wide", None),
            P("wide", None),
            P("wide", None),
            P("wide", None),
            P(),
            P("wide", None),
            P("wide", None),
            P("wide", None),
        ),
        check_vma=False,
    )
```

profile of v0, /device:TPU:0, one launch (start us, length us, event | category | flops | bytes accessed | tf_op | source)
XLA Modules:
  0.0 2421.2 jit_solution(15811180874852004695)
XLA Ops:
  11.4 76.4 %all-gather.17.cloned.1.call-done = bf16[2048,2048]{1,0:T(8,128)(2,1)} async-done(((bf16[128,2048]{1,0:T(8,128)(2,1)}), bf16[2048,2048]{1,0:T(8,128)(2,1)}) %all-gather.17.cloned.1.call-update) | async-done | bytes 8388624 | tf_op jit(solution)/shard_map/all_gather | solution.py:116
  87.8 12.5 copy.64
  107.4 55.7 %all-gather.11.cloned.1.call-done = bf16[2048,2048]{1,0:T(8,128)(2,1)} async-done(((bf16[128,2048]{1,0:T(8,128)(2,1)}), bf16[2048,2048]{1,0:T(8,128)(2,1)}) %all-gather.11.cloned.1.call-update) | async-done | bytes 8388624 | tf_op jit(solution)/shard_map/all_gather | solution.py:115
  163.2 12.4 copy.61
  175.6 62.9 %all-gather.15.cloned.1.call-done = bf16[2048,2048]{1,0:T(8,128)(2,1)} async-done(((bf16[128,2048]{1,0:T(8,128)(2,1)}), bf16[2048,2048]{1,0:T(8,128)(2,1)}) %all-gather.15.cloned.1.call-update) | async-done | bytes 8388624 | tf_op jit(solution)/shard_map/all_gather | solution.py:114
  238.5 12.4 copy.63
  264.3 50.0 %all-gather.19.cloned.1.call-done = bf16[2048,2048]{1,0:T(8,128)(2,1)} async-done(((bf16[128,2048]{1,0:T(8,128)(2,1)}), bf16[2048,2048]{1,0:T(8,128)(2,1)}) %all-gather.19.cloned.1.call-update) | async-done | bytes 8388624 | tf_op jit(solution)/shard_map/all_gather | solution.py:174
  314.3 11.6 copy.67
  325.9 64.2 %all-gather.13.cloned.1.call-done = bf16[2048,2048]{1,0:T(8,128)(2,1)} async-done(((bf16[128,2048]{1,0:T(8,128)(2,1)}), bf16[2048,2048]{1,0:T(8,128)(2,1)}) %all-gather.13.cloned.1.call-update) | async-done | bytes 8388624 | tf_op jit(solution)/shard_map/all_gather | solution.py:173
  402.7 18.2 while.47
  423.0 42.2 %all-gather.21.cloned.1.call-done = bf16[2048,2048]{1,0:T(8,128)(2,1)} async-done(((bf16[128,2048]{1,0:T(8,128)(2,1)}), bf16[2048,2048]{1,0:T(8,128)(2,1)}) %all-gather.21.cloned.1.call-update) | async-done | bytes 8388624 | tf_op jit(solution)/shard_map/all_gather | solution.py:117
  474.9 70.5 %all-gather.23.cloned.1.call-done = bf16[2048,2048]{1,0:T(8,128)(2,1)} async-done(((bf16[128,2048]{1,0:T(8,128)(2,1)}), bf16[2048,2048]{1,0:T(8,128)(2,1)}) %all-gather.23.cloned.1.call-update) | async-done | bytes 8388624 | tf_op jit(solution)/shard_map/all_gather | solution.py:189
  562.6 58.7 %all-gather.25.cloned.1.call-done = bf16[2048,2048]{1,0:T(8,128)(2,1)} async-done(((bf16[128,2048]{1,0:T(8,128)(2,1)}), bf16[2048,2048]{1,0:T(8,128)(2,1)}) %all-gather.25.cloned.1.call-update) | async-done | bytes 8388624 | tf_op jit(solution)/shard_map/all_gather | solution.py:202
  621.3 12.2 multiply_convert_fusion.6
  642.0 11.8 convolution_add_fusion
  653.8 12.0 fusion.110
  668.3 162.5 %reduce-scatter.6.cloned.1.call-done = f32[128,2048]{1,0:T(8,128)} async-done(((f32[2048,2048]{1,0:T(8,128)}), f32[128,2048]{1,0:T(8,128)}) %reduce-scatter.6.cloned.1.call-update) | async-done | bytes 1048592 | tf_op jit(solution)/shard_map/reduce_scatter | solution.py:205
  833.0 179.4 %reduce-scatter.4.cloned.1.call-done = f32[128,2048]{1,0:T(8,128)} async-done(((f32[2048,2048]{1,0:T(8,128)}), f32[128,2048]{1,0:T(8,128)}) %reduce-scatter.4.cloned.1.call-update) | async-done | bytes 1048592 | tf_op jit(solution)/shard_map/reduce_scatter | solution.py:193
  1023.2 65.9 %all-gather.27.cloned.1.call-done = bf16[2048,2048]{1,0:T(8,128)(2,1)} async-done(((bf16[128,2048]{1,0:T(8,128)(2,1)}), bf16[2048,2048]{1,0:T(8,128)(2,1)}) %all-gather.27.cloned.1.call-update) | async-done | bytes 8388624 | tf_op jit(solution)/shard_map/all_gather | solution.py:291
  1100.7 20.8 all_gather.47
  1124.8 19.6 all_gather.49
  1146.3 26.4 %while.48 = (s32[]{:T(128)}, f32[128,32,64]{0,2,1:T(8,128)}, s32[4]{0:T(128)S(1)}, s32[]{:T(128)}, s32[]{:T(128)}, /*index=5*/bf16[4,512,2048]{1,2,0:T(8,128)(2,...) while((s32[]{:T(128)}, f32[128,32,64]{0,2,1:T(8,128)}, ...), condition=%wide.region_15.16_spmd.clone, body=%wide.region_12.15_spmd.clone.sunk | while | flops 820381312 | bytes 34774328 | solution.py:80
  1148.2 18.6 conditional.11
  1195.9 115.9 %while.49 = (s32[]{:T(128)}, f32[128,32,64]{0,2,1:T(8,128)}, f32[128,32,64]{0,2,1:T(8,128)}, s32[4]{0:T(128)S(1)}, s32[]{:T(128)}, /*index=5*/pred[]{:T(512)}, s...) while((s32[]{:T(128)}, f32[128,32,64]{0,2,1:T(8,128)}, ...), condition=%wide.region_19.20_spmd.clone.clone, body=%wide.region_16.19_spmd.clone.clone.sunk | while | flops 1097466624 | bytes 47848052 | solution.py:80
  1197.5 27.6 %conditional.12 = ((f32[128,32,64]{0,2,1:T(8,128)}, f32[128,32,64]{0,2,1:T(8,128)})) conditional(s32[]{:T(128)} %convert_element_type.343, (f32[128,32,64]{0,2,1:T(8,128)}, f32[128,32,64]{0,2,1:T(8,128)}) %tuple.169, (s32[]{:T(128)}, s32[]{:T(128)}, s32[]{:T(128)}, bf16[4,512,2048]{1,2,0:T(8,128)(2,1)}, s32[]{:T(128)}, ...), branch_computations={%region_17.17_spmd, %region_18.18_spmd} | conditional | flops 1097466624 | bytes 47847212 | solution.py:78
  1226.4 27.6 %conditional.12 = ((f32[128,32,64]{0,2,1:T(8,128)}, f32[128,32,64]{0,2,1:T(8,128)})) conditional(s32[]{:T(128)} %convert_element_type.343, (f32[128,32,64]{0,2,1:T(8,128)}, f32[128,32,64]{0,2,1:T(8,128)}) %tuple.169, (s32[]{:T(128)}, s32[]{:T(128)}, s32[]{:T(128)}, bf16[4,512,2048]{1,2,0:T(8,128)(2,1)}, s32[]{:T(128)}, ...), branch_computations={%region_17.17_spmd, %region_18.18_spmd} | conditional | flops 1097466624 | bytes 47847212 | solution.py:78
  1255.2 27.6 %conditional.12 = ((f32[128,32,64]{0,2,1:T(8,128)}, f32[128,32,64]{0,2,1:T(8,128)})) conditional(s32[]{:T(128)} %convert_element_type.343, (f32[128,32,64]{0,2,1:T(8,128)}, f32[128,32,64]{0,2,1:T(8,128)}) %tuple.169, (s32[]{:T(128)}, s32[]{:T(128)}, s32[]{:T(128)}, bf16[4,512,2048]{1,2,0:T(8,128)(2,1)}, s32[]{:T(128)}, ...), branch_computations={%region_17.17_spmd, %region_18.18_spmd} | conditional | flops 1097466624 | bytes 47847212 | solution.py:78
  1284.0 27.6 %conditional.12 = ((f32[128,32,64]{0,2,1:T(8,128)}, f32[128,32,64]{0,2,1:T(8,128)})) conditional(s32[]{:T(128)} %convert_element_type.343, (f32[128,32,64]{0,2,1:T(8,128)}, f32[128,32,64]{0,2,1:T(8,128)}) %tuple.169, (s32[]{:T(128)}, s32[]{:T(128)}, s32[]{:T(128)}, bf16[4,512,2048]{1,2,0:T(8,128)(2,1)}, s32[]{:T(128)}, ...), branch_computations={%region_17.17_spmd, %region_18.18_spmd} | conditional | flops 1097466624 | bytes 47847212 | solution.py:78
  1336.2 39.9 %pad_maximum_fusion = f32[2048,8192]{0,1:T(8,128)} fusion(f32[2048,2048]{0,1:T(8,128)} %fusion.95, f32[2048,2048]{0,1:T(8,128)S(1)} %fusion.93, f32[2048,2048]{0,1:T(8,128)} %fusion.89, f32[2048,2048]{0,1:T(8,128)} %fusion.91), kind=kLoop, calls=%fused_computation.68 | loop fusion | flops 50331648 | bytes 134217728 | tf_op jit(solution)/shard_map/concatenate | solution.py:318
  1405.3 606.1 %reduce-scatter.8.cloned.1.call-done = f32[128,8192]{0,1:T(8,128)} async-done(((f32[2048,8192]{0,1:T(8,128)}), f32[128,8192]{0,1:T(8,128)}) %reduce-scatter.8.cloned.1.call-update) | async-done | bytes 4194320 | tf_op jit(solution)/shard_map/reduce_scatter | solution.py:317
  2028.5 39.1 %all-reduce = (f32[2048]{0:T(1024)}, f32[2048]{0:T(1024)}) all-reduce(f32[2048]{0:T(1024)S(1)} %get-tuple-element.985, f32[2048]{0:T(1024)S(1)} %copy-done.29), channel_id=1, replica_groups=mesh['narrow'=2,'wide'=16] {'narrow','wide'}, use_global_device_ids=true, to_apply=%region_22.23 | all-reduce | flops 4096 | bytes 32768 | tf_op jit(solution)/shard_map/psum | solution.py:331
  2068.9 326.6 %all-reduce.4.cloned.1.call-done = (f32[128,8192]{0,1:T(8,128)}, f32[512,2048]{1,0:T(8,128)}, f32[512,2048]{1,0:T(8,128)}, f32[512,2048]{1,0:T(8,128)}) async-done(((f32[128,8192]{0,1:T(8,128)}, f32[512,2048]{1,0:T(8,128)}, f32[512,2048]{1,0:T(8,128)}, f32[512,2048]{1,0:T(8,128)}), (f32[128,8192]{0,1:T(8,128)}, f32[512,2048]{1,0:T(8,128)}, f32[512,2048]{1,0:T(8,128)}, ...) | async-done | bytes 16777232 | tf_op jit(solution)/shard_map/psum | solution.py:332
  (265 shorter events, 376.8 us)
Async XLA Ops:
  7.2 614.1 %copy-start = (bf16[512,2048]{1,0:T(8,128)(2,1)S(1)}, bf16[512,2048]{1,0:T(8,128)(2,1)}, u32[]{:S(2)}) copy-start(bf16[512,2048]{1,0:T(8,128)(2,1)} %param.34) | copy-start | bytes 6291460
  7.2 80.6 %all-gather.17.cloned.1.call-start = ((), (), s32[]{:S(2)}) async-start(), calls=%async_computation.6 | async-start | bytes 8912896 | tf_op jit(solution)/shard_map/all_gather | solution.py:116
  7.9 155.2 %all-gather.11.cloned.1.call-start = ((), (), s32[]{:S(2)}) async-start(), calls=%async_computation.3 | async-start | bytes 8912896 | tf_op jit(solution)/shard_map/all_gather | solution.py:115
  8.7 229.8 %all-gather.15.cloned.1.call-start = ((), (), s32[]{:S(2)}) async-start(), calls=%async_computation.5 | async-start | bytes 8912896 | tf_op jit(solution)/shard_map/all_gather | solution.py:114
  9.4 304.9 %all-gather.19.cloned.1.call-start = ((), (), s32[]{:S(2)}) async-start(), calls=%async_computation.7 | async-start | bytes 8912896 | tf_op jit(solution)/shard_map/all_gather | solution.py:174
  10.1 246.7 %copy-start.21 = (f32[2048]{0:T(1024)}, f32[2048]{0:T(1024)S(1)}, u32[]{:S(2)}) copy-start(f32[2048]{0:T(1024)S(1)} %convert_element_type.180) | copy-start | bytes 24580
  11.4 245.5 %copy-start.27 = (f32[128]{0:T(128)}, f32[128]{0:T(128)S(1)}, u32[]{:S(2)}) copy-start(f32[128]{0:T(128)S(1)} %add_rsqrt_fusion.1) | copy-start | bytes 1540
  87.8 12.5 copy-start.2
  106.1 69.4 %copy-start.19 = (bf16[128,32,64]{0,2,1:T(8,128)(2,1)}, bf16[128,32,64]{0,2,1:T(8,128)(2,1)S(1)}, u32[]{:S(2)}) copy-start(bf16[128,32,64]{0,2,1:T(8,128)(2,1)S(1)} %convolution_convert_fusion.1) | copy-start | bytes 1572868
  107.2 282.8 %all-gather.13.cloned.1.call-start = ((), (), s32[]{:S(2)}) async-start(), calls=%async_computation.4 | async-start | bytes 8912896 | tf_op jit(solution)/shard_map/all_gather | solution.py:173
  107.4 152.3 %copy-start.23 = (f32[128,64]{0,1:T(8,128)}, f32[128,64]{0,1:T(8,128)S(1)}, u32[]{:S(2)}) copy-start(f32[128,64]{0,1:T(8,128)S(1)} %get-tuple-element.1109) | copy-start | bytes 98308
  107.4 152.3 %copy-start.25 = (f32[128,64]{0,1:T(8,128)}, f32[128,64]{0,1:T(8,128)S(1)}, u32[]{:S(2)}) copy-start(f32[128,64]{0,1:T(8,128)S(1)} %get-tuple-element.1110) | copy-start | bytes 98308
  263.1 202.1 %all-gather.21.cloned.1.call-start = ((), (), s32[]{:S(2)}) async-start(), calls=%async_computation.8 | async-start | bytes 8912896 | tf_op jit(solution)/shard_map/all_gather | solution.py:117
  263.7 281.7 %all-gather.23.cloned.1.call-start = ((), (), s32[]{:S(2)}) async-start(), calls=%async_computation.9 | async-start | bytes 8912896 | tf_op jit(solution)/shard_map/all_gather | solution.py:189
  472.1 149.2 %all-gather.25.cloned.1.call-start = ((), (), s32[]{:S(2)}) async-start(), calls=%async_computation.11 | async-start | bytes 8912896 | tf_op jit(solution)/shard_map/all_gather | solution.py:202
  474.8 356.0 %reduce-scatter.6.cloned.1.call-start = ((), (), s32[]{:S(2)}) async-start(), calls=%async_computation.12 | async-start | bytes 17825792 | tf_op jit(solution)/shard_map/reduce_scatter | solution.py:205
  621.3 12.3 copy-start.33
  653.8 358.6 %reduce-scatter.4.cloned.1.call-start = ((), (), s32[]{:S(2)}) async-start(), calls=%async_computation.10 | async-start | bytes 17825792 | tf_op jit(solution)/shard_map/reduce_scatter | solution.py:193
  665.9 164.9 %copy-start.7 = (f32[128,2048]{1,0:T(8,128)S(1)}, f32[128,2048]{1,0:T(8,128)}, u32[]{:S(2)}) copy-start(f32[128,2048]{1,0:T(8,128)} %copy-done.6) | copy-start | bytes 3145732
  665.9 423.1 %all-gather.27.cloned.1.call-start = ((), (), s32[]{:S(2)}) async-start(), calls=%async_computation.13 | async-start | bytes 8912896 | tf_op jit(solution)/shard_map/all_gather | solution.py:291
  667.2 514.9 %all-gather.29.cloned.1.call-start = ((), (), s32[]{:S(2)}) async-start(), calls=%async_computation.14 | async-start | bytes 8912896 | tf_op jit(solution)/shard_map/all_gather | solution.py:292
  1015.3 85.4 %copy-start.8 = (f32[128,2048]{1,0:T(8,128)}, f32[128,2048]{1,0:T(8,128)S(1)}, u32[]{:S(2)}) copy-start(f32[128,2048]{1,0:T(8,128)S(1)} %get-tuple-element.1090) | copy-start | bytes 3145732
  1023.1 988.2 %reduce-scatter.8.cloned.1.call-start = ((), (), s32[]{:S(2)}) async-start(), calls=%async_computation.15 | async-start | bytes 71303168 | tf_op jit(solution)/shard_map/reduce_scatter | solution.py:317
  1089.0 33.1 %copy-start.11 = (bf16[128,2048]{1,0:T(8,128)(2,1)S(1)}, bf16[128,2048]{1,0:T(8,128)(2,1)}, u32[]{:S(2)}) copy-start(bf16[128,2048]{1,0:T(8,128)(2,1)} %get-tuple-element.1107) | copy-start | bytes 1572868
  1182.1 13.8 copy-start.5
  1182.1 13.8 copy-start.20
  1195.8 117.3 %copy-start.26 = (f32[128,64]{0,1:T(8,128)S(1)}, f32[128,64]{0,1:T(8,128)}, u32[]{:S(2)}) copy-start(f32[128,64]{0,1:T(8,128)} %copy-done.25) | copy-start | bytes 98308
  1376.1 1019.3 %all-reduce.4.cloned.1.call-start = ((), (), s32[]{:S(2)}) async-start(), calls=%async_computation.16 | async-start | bytes 33554432 | tf_op jit(solution)/shard_map/psum | solution.py:332
  1376.2 11.6 copy-start.17
  1376.2 23.1 slice-start.2
  2011.4 14.0 slice-start
  2025.4 42.2 %copy-start.9 = (f32[128,2048]{1,0:T(8,128)S(1)}, f32[128,2048]{1,0:T(8,128)}, u32[]{:S(2)}) copy-start(f32[128,2048]{1,0:T(8,128)} %copy-done.8) | copy-start | bytes 3145732
  (22 other events, 136.4 us)
Sparse Core Ops, SparseCore 0:
  10.2 77.5 all-gather.16
  90.0 73.1 all-gather.10
  165.3 73.1 all-gather.14
  241.1 73.1 all-gather.18
  316.8 73.1 all-gather.12
  392.0 73.1 all-gather.20
  472.2 73.1 all-gather.22
  548.1 73.1 all-gather.24
  653.9 176.8 reduce-scatter.5
  834.8 177.5 reduce-scatter.3
  1015.1 73.8 all-gather.26
  1091.1 76.0 all-gather.28
  1376.2 635.0 reduce-scatter.7
  2014.4 381.0 all-reduce.3
where the time goes:
time: 2430 us; the launch traced here: 2420 us
  waiting for transfers between devices  1820 us (75%)
  matrix products  270 us (11%)
  local copies, waits for them, and re-layouts  149 us (6%)
  blocking collectives  79.5 us (3%)
  other arithmetic  67.5 us (3%)
    reduce_scatter x1, waiting for transfers between devices, shards(): lax.psum_scatter(jnp.concatenate([contract_rows(norm_one, query_lin_back)...  606 us
    psum x1, waiting for transfers between devices, shards(): summed = lax.psum((attention_part, gate_part, up_part, down_part), 'narrow')  327 us
    reduce_scatter x1, waiting for transfers between devices, shards(): lax.psum_scatter(jnp.dot(hidden, w_down, preferred_element_type=jnp.float...  179 us
    reduce_scatter x1, waiting for transfers between devices, shards(): lax.psum_scatter(jnp.dot(gate_back, w_gate, preferred_element_type=jnp.fl...  163 us
    all_gather x1, waiting for transfers between devices, shards(): lax.all_gather(w_value, 'wide', axis=0, tiled=True)  76.4 us
    all_gather x1, waiting for transfers between devices, shards(): group_norm = lax.all_gather(norm_two, 'wide', axis=0, tiled=True)  70.5 us
    all_gather x1, waiting for transfers between devices, shards(): lax.all_gather(query_wire, 'wide', axis=0, tiled=True)  65.9 us
    all_gather x1, waiting for transfers between devices, shards(): lax.all_gather(key_flat, 'wide', axis=0, tiled=True)  64.2 us
  transfers between devices with their start and end apart: 14, of which 13 were waited for; matrix products, arithmetic and copies ran while one was open for 10% of the time, Pallas kernels for 0%

commit v1 on v0

--- a/solution.py
+++ b/solution.py
@@ -186,7 +186,12 @@
     factor_two = rms_factor(residual)
     normed_two = residual * factor_two
     norm_two = (normed_two * gain_two).astype(jnp.bfloat16)
-    group_norm = lax.all_gather(norm_two, "wide", axis=0, tiled=True)
+    ring = [norm_two]
+    for hop in range(15):
+        ring.append(lax.ppermute(ring[-1], "wide", [(dev, (dev + 1) % 16) for dev in range(16)]))
+    group_norm = jnp.roll(
+        jnp.concatenate(ring[::-1], axis=0), (lax.axis_index("wide") + 1) * ring[0].shape[0], axis=0
+    )
     gate_proj = contract_cols(group_norm, w_gate)
     up_proj = contract_cols(group_norm, w_up)
     hidden = (jax.nn.silu(gate_proj) * up_proj).astype(jnp.bfloat16)

time: 2430 us -> 2530 us (1.041)
  waiting for transfers between devices: 1820 us -> 1880 us
  local copies, waits for them, and re-layouts: 149 us -> 192 us
    ppermute x0 -> x15, waiting for transfers between devices: none -> 191 us  [shards(): lax.ppermute(ring[-1], 'wide', [(dev, (dev + 1) % 16) for dev in range(16)])]
    all_gather x1 -> x0, waiting for transfers between devices: 70.5 us -> none  [shards(): group_norm = lax.all_gather(norm_two, 'wide', axis=0, tiled=True)]
    all_gather x1, waiting for transfers between devices: 58.7 us -> 0.01 us  [shards(): group_back = lax.all_gather(mlp_back, 'wide', axis=0, tiled=True)]
    unnamed x87 -> x163, local copies, waits for them, and re-layouts: 63 us -> 106 us
  transfers between devices with their start and end apart: 14 -> 28, of which waited for: 13 -> 26; matrix products, arithmetic and copies ran while one was open for 10% -> 9% of each run, Pallas kernels for 0% -> 0%
where the time goes in v1:
time: 2530 us; the launch traced here: 2520 us
  waiting for transfers between devices  1880 us (74%)
  matrix products  269 us (11%)
  local copies, waits for them, and re-layouts  192 us (8%)
  blocking collectives  79.2 us (3%)
  other arithmetic  68.7 us (3%)
    reduce_scatter x1, waiting for transfers between devices, shards(): lax.psum_scatter(jnp.concatenate([contract_rows(norm_one, query_lin_back)...  606 us
    psum x1, waiting for transfers between devices, shards(): summed = lax.psum((attention_part, gate_part, up_part, down_part), 'narrow')  327 us
    ppermute x15, waiting for transfers between devices, shards(): lax.ppermute(ring[-1], 'wide', [(dev, (dev + 1) % 16) for dev in range(16)])  191 us
    reduce_scatter x1, waiting for transfers between devices, shards(): lax.psum_scatter(jnp.dot(hidden, w_down, preferred_element_type=jnp.float...  180 us
    reduce_scatter x1, waiting for transfers between devices, shards(): lax.psum_scatter(jnp.dot(gate_back, w_gate, preferred_element_type=jnp.fl...  163 us
    unnamed x163, local copies, waits for them, and re-layouts  106 us
    all_gather x1, waiting for transfers between devices, shards(): lax.all_gather(w_value, 'wide', axis=0, tiled=True)  76.4 us
    all_gather x1, waiting for transfers between devices, shards(): lax.all_gather(query_wire, 'wide', axis=0, tiled=True)  65.7 us
  transfers between devices with their start and end apart: 28, of which 26 were waited for; matrix products, arithmetic and copies ran while one was open for 9% of the time, Pallas kernels for 0%

profile of v1, /device:TPU:0, one launch (start us, length us, event | category | flops | bytes accessed | tf_op | source)
XLA Modules:
  0.0 2524.0 jit_solution(11219789414133958152)
XLA Ops:
  11.4 76.4 %all-gather.16.cloned.1.call-done = bf16[2048,2048]{1,0:T(8,128)(2,1)} async-done(((bf16[128,2048]{1,0:T(8,128)(2,1)}), bf16[2048,2048]{1,0:T(8,128)(2,1)}) %all-gather.16.cloned.1.call-update) | async-done | bytes 8388624 | tf_op jit(solution)/shard_map/all_gather | solution.py:116
  87.8 12.4 copy.64
  107.4 55.8 %all-gather.10.cloned.1.call-done = bf16[2048,2048]{1,0:T(8,128)(2,1)} async-done(((bf16[128,2048]{1,0:T(8,128)(2,1)}), bf16[2048,2048]{1,0:T(8,128)(2,1)}) %all-gather.10.cloned.1.call-update) | async-done | bytes 8388624 | tf_op jit(solution)/shard_map/all_gather | solution.py:115
  163.2 12.3 copy.61
  175.5 63.0 %all-gather.14.cloned.1.call-done = bf16[2048,2048]{1,0:T(8,128)(2,1)} async-done(((bf16[128,2048]{1,0:T(8,128)(2,1)}), bf16[2048,2048]{1,0:T(8,128)(2,1)}) %all-gather.14.cloned.1.call-update) | async-done | bytes 8388624 | tf_op jit(solution)/shard_map/all_gather | solution.py:114
  238.5 12.4 copy.63
  267.1 47.1 %all-gather.18.cloned.1.call-done = bf16[2048,2048]{1,0:T(8,128)(2,1)} async-done(((bf16[128,2048]{1,0:T(8,128)(2,1)}), bf16[2048,2048]{1,0:T(8,128)(2,1)}) %all-gather.18.cloned.1.call-update) | async-done | bytes 8388624 | tf_op jit(solution)/shard_map/all_gather | solution.py:174
  325.8 64.2 %all-gather.12.cloned.1.call-done = bf16[2048,2048]{1,0:T(8,128)(2,1)} async-done(((bf16[128,2048]{1,0:T(8,128)(2,1)}), bf16[2048,2048]{1,0:T(8,128)(2,1)}) %all-gather.12.cloned.1.call-update) | async-done | bytes 8388624 | tf_op jit(solution)/shard_map/all_gather | solution.py:173
  402.7 18.2 while.47
  423.0 42.2 %all-gather.20.cloned.1.call-done = bf16[2048,2048]{1,0:T(8,128)(2,1)} async-done(((bf16[128,2048]{1,0:T(8,128)(2,1)}), bf16[2048,2048]{1,0:T(8,128)(2,1)}) %all-gather.20.cloned.1.call-update) | async-done | bytes 8388624 | tf_op jit(solution)/shard_map/all_gather | solution.py:117
  471.6 16.2 collective-permute-done
  487.8 17.4 collective-permute-done.1
  506.1 22.3 collective-permute-done.2
  529.2 20.8 collective-permute-done.3
  659.0 11.6 collective-permute-done.13
  756.4 11.9 fusion.120
  770.6 163.0 %reduce-scatter.6.cloned.1.call-done = f32[128,2048]{1,0:T(8,128)} async-done(((f32[2048,2048]{1,0:T(8,128)}), f32[128,2048]{1,0:T(8,128)}) %reduce-scatter.6.cloned.1.call-update) | async-done | bytes 1048592 | tf_op jit(solution)/shard_map/reduce_scatter | solution.py:210
  935.8 179.5 %reduce-scatter.4.cloned.1.call-done = f32[128,2048]{1,0:T(8,128)} async-done(((f32[2048,2048]{1,0:T(8,128)}), f32[128,2048]{1,0:T(8,128)}) %reduce-scatter.4.cloned.1.call-update) | async-done | bytes 1048592 | tf_op jit(solution)/shard_map/reduce_scatter | solution.py:198
  1126.1 65.7 %all-gather.24.cloned.1.call-done = bf16[2048,2048]{1,0:T(8,128)(2,1)} async-done(((bf16[128,2048]{1,0:T(8,128)(2,1)}), bf16[2048,2048]{1,0:T(8,128)(2,1)}) %all-gather.24.cloned.1.call-update) | async-done | bytes 8388624 | tf_op jit(solution)/shard_map/all_gather | solution.py:296
  1203.4 20.7 all_gather.43
  1227.5 19.6 all_gather.45
  1249.0 26.3 %while.48 = (s32[]{:T(128)}, f32[128,32,64]{0,2,1:T(8,128)}, s32[4]{0:T(128)S(1)}, s32[]{:T(128)}, s32[]{:T(128)}, /*index=5*/bf16[4,512,2048]{1,2,0:T(8,128)(2,...) while((s32[]{:T(128)}, f32[128,32,64]{0,2,1:T(8,128)}, ...), condition=%wide.region_15.16_spmd.clone, body=%wide.region_12.15_spmd.clone.sunk | while | flops 820381312 | bytes 34774328 | solution.py:80
  1250.9 18.6 conditional.11
  1298.5 115.8 %while.49 = (s32[]{:T(128)}, f32[128,32,64]{0,2,1:T(8,128)}, f32[128,32,64]{0,2,1:T(8,128)}, s32[4]{0:T(128)S(1)}, s32[]{:T(128)}, /*index=5*/pred[]{:T(512)}, s...) while((s32[]{:T(128)}, f32[128,32,64]{0,2,1:T(8,128)}, ...), condition=%wide.region_19.20_spmd.clone.clone, body=%wide.region_16.19_spmd.clone.clone.sunk | while | flops 1097466624 | bytes 47848052 | solution.py:80
  1300.0 27.6 %conditional.12 = ((f32[128,32,64]{0,2,1:T(8,128)}, f32[128,32,64]{0,2,1:T(8,128)})) conditional(s32[]{:T(128)} %convert_element_type.347, (f32[128,32,64]{0,2,1:T(8,128)}, f32[128,32,64]{0,2,1:T(8,128)}) %tuple.169, (s32[]{:T(128)}, s32[]{:T(128)}, s32[]{:T(128)}, bf16[4,512,2048]{1,2,0:T(8,128)(2,1)}, s32[]{:T(128)}, ...), branch_computations={%region_17.17_spmd, %region_18.18_spmd} | conditional | flops 1097466624 | bytes 47847212 | solution.py:78
  1328.8 27.6 %conditional.12 = ((f32[128,32,64]{0,2,1:T(8,128)}, f32[128,32,64]{0,2,1:T(8,128)})) conditional(s32[]{:T(128)} %convert_element_type.347, (f32[128,32,64]{0,2,1:T(8,128)}, f32[128,32,64]{0,2,1:T(8,128)}) %tuple.169, (s32[]{:T(128)}, s32[]{:T(128)}, s32[]{:T(128)}, bf16[4,512,2048]{1,2,0:T(8,128)(2,1)}, s32[]{:T(128)}, ...), branch_computations={%region_17.17_spmd, %region_18.18_spmd} | conditional | flops 1097466624 | bytes 47847212 | solution.py:78
  1357.6 27.6 %conditional.12 = ((f32[128,32,64]{0,2,1:T(8,128)}, f32[128,32,64]{0,2,1:T(8,128)})) conditional(s32[]{:T(128)} %convert_element_type.347, (f32[128,32,64]{0,2,1:T(8,128)}, f32[128,32,64]{0,2,1:T(8,128)}) %tuple.169, (s32[]{:T(128)}, s32[]{:T(128)}, s32[]{:T(128)}, bf16[4,512,2048]{1,2,0:T(8,128)(2,1)}, s32[]{:T(128)}, ...), branch_computations={%region_17.17_spmd, %region_18.18_spmd} | conditional | flops 1097466624 | bytes 47847212 | solution.py:78
  1386.4 27.6 %conditional.12 = ((f32[128,32,64]{0,2,1:T(8,128)}, f32[128,32,64]{0,2,1:T(8,128)})) conditional(s32[]{:T(128)} %convert_element_type.347, (f32[128,32,64]{0,2,1:T(8,128)}, f32[128,32,64]{0,2,1:T(8,128)}) %tuple.169, (s32[]{:T(128)}, s32[]{:T(128)}, s32[]{:T(128)}, bf16[4,512,2048]{1,2,0:T(8,128)(2,1)}, s32[]{:T(128)}, ...), branch_computations={%region_17.17_spmd, %region_18.18_spmd} | conditional | flops 1097466624 | bytes 47847212 | solution.py:78
  1438.7 40.0 %pad_maximum_fusion = f32[2048,8192]{0,1:T(8,128)} fusion(f32[2048,2048]{0,1:T(8,128)} %fusion.103, f32[2048,2048]{0,1:T(8,128)S(1)} %fusion.101, f32[2048,2048]{0,1:T(8,128)} %fusion.97, f32[2048,2048]{0,1:T(8,128)} %fusion.99), kind=kLoop, calls=%fused_computation.68 | loop fusion | flops 50331648 | bytes 134217728 | tf_op jit(solution)/shard_map/concatenate | solution.py:323
  1507.6 606.3 %reduce-scatter.8.cloned.1.call-done = f32[128,8192]{0,1:T(8,128)} async-done(((f32[2048,8192]{0,1:T(8,128)}), f32[128,8192]{0,1:T(8,128)}) %reduce-scatter.8.cloned.1.call-update) | async-done | bytes 4194320 | tf_op jit(solution)/shard_map/reduce_scatter | solution.py:322
  2131.1 38.9 %all-reduce = (f32[2048]{0:T(1024)}, f32[2048]{0:T(1024)}) all-reduce(f32[2048]{0:T(1024)S(1)} %get-tuple-element.985, f32[2048]{0:T(1024)S(1)} %copy-done.51), channel_id=1, replica_groups=mesh['narrow'=2,'wide'=16] {'narrow','wide'}, use_global_device_ids=true, to_apply=%region_22.23 | all-reduce | flops 4096 | bytes 32768 | tf_op jit(solution)/shard_map/psum | solution.py:336
  2171.3 326.9 %all-reduce.4.cloned.1.call-done = (f32[128,8192]{0,1:T(8,128)}, f32[512,2048]{1,0:T(8,128)}, f32[512,2048]{1,0:T(8,128)}, f32[512,2048]{1,0:T(8,128)}) async-done(((f32[128,8192]{0,1:T(8,128)}, f32[512,2048]{1,0:T(8,128)}, f32[512,2048]{1,0:T(8,128)}, f32[512,2048]{1,0:T(8,128)}), (f32[128,8192]{0,1:T(8,128)}, f32[512,2048]{1,0:T(8,128)}, f32[512,2048]{1,0:T(8,128)}, ...) | async-done | bytes 16777232 | tf_op jit(solution)/shard_map/psum | solution.py:337
  (370 shorter events, 558.1 us)
Async XLA Ops:
  7.2 716.4 %copy-start = (bf16[512,2048]{1,0:T(8,128)(2,1)S(1)}, bf16[512,2048]{1,0:T(8,128)(2,1)}, u32[]{:S(2)}) copy-start(bf16[512,2048]{1,0:T(8,128)(2,1)} %param.32) | copy-start | bytes 6291460
  7.2 80.6 %all-gather.16.cloned.1.call-start = ((), (), s32[]{:S(2)}) async-start(), calls=%async_computation.6 | async-start | bytes 8912896 | tf_op jit(solution)/shard_map/all_gather | solution.py:116
  7.9 155.2 %all-gather.10.cloned.1.call-start = ((), (), s32[]{:S(2)}) async-start(), calls=%async_computation.3 | async-start | bytes 8912896 | tf_op jit(solution)/shard_map/all_gather | solution.py:115
  8.7 229.8 %all-gather.14.cloned.1.call-start = ((), (), s32[]{:S(2)}) async-start(), calls=%async_computation.5 | async-start | bytes 8912896 | tf_op jit(solution)/shard_map/all_gather | solution.py:114
  9.4 304.9 %all-gather.18.cloned.1.call-start = ((), (), s32[]{:S(2)}) async-start(), calls=%async_computation.7 | async-start | bytes 8912896 | tf_op jit(solution)/shard_map/all_gather | solution.py:174
  10.1 246.7 %copy-start.43 = (f32[2048]{0:T(1024)}, f32[2048]{0:T(1024)S(1)}, u32[]{:S(2)}) copy-start(f32[2048]{0:T(1024)S(1)} %convert_element_type.180) | copy-start | bytes 24580
  11.4 245.5 %copy-start.49 = (f32[128]{0:T(128)}, f32[128]{0:T(128)S(1)}, u32[]{:S(2)}) copy-start(f32[128]{0:T(128)S(1)} %add_rsqrt_fusion.1) | copy-start | bytes 1540
  107.1 282.9 %all-gather.12.cloned.1.call-start = ((), (), s32[]{:S(2)}) async-start(), calls=%async_computation.4 | async-start | bytes 8912896 | tf_op jit(solution)/shard_map/all_gather | solution.py:173
  263.1 202.1 %all-gather.20.cloned.1.call-start = ((), (), s32[]{:S(2)}) async-start(), calls=%async_computation.8 | async-start | bytes 8912896 | tf_op jit(solution)/shard_map/all_gather | solution.py:117
  263.7 407.0 %all-gather.22.cloned.1.call-start = ((), (), s32[]{:S(2)}) async-start(), calls=%async_computation.10 | async-start | bytes 8912896 | tf_op jit(solution)/shard_map/all_gather | solution.py:207
  266.9 666.7 %reduce-scatter.6.cloned.1.call-start = ((), (), s32[]{:S(2)}) async-start(), calls=%async_computation.11 | async-start | bytes 17825792 | tf_op jit(solution)/shard_map/reduce_scatter | solution.py:210
  471.3 16.5 collective-permute-start
  487.8 17.4 collective-permute-start.1
  506.1 22.3 collective-permute-start.2
  529.2 20.8 collective-permute-start.3
  550.8 11.3 collective-permute-start.4
  562.9 11.3 collective-permute-start.5
  575.1 11.3 collective-permute-start.6
  587.2 11.3 collective-permute-start.7
  599.2 11.3 collective-permute-start.8
  611.3 11.3 collective-permute-start.9
  623.4 11.3 collective-permute-start.10
  635.5 11.3 collective-permute-start.11
  647.6 11.4 collective-permute-start.12
  659.0 11.6 collective-permute-start.13
  670.6 11.6 collective-permute-start.14
  754.8 360.5 %reduce-scatter.4.cloned.1.call-start = ((), (), s32[]{:S(2)}) async-start(), calls=%async_computation.9 | async-start | bytes 17825792 | tf_op jit(solution)/shard_map/reduce_scatter | solution.py:198
  768.3 347.0 %copy-start.54 = (f32[128]{0:T(128)S(1)}, f32[128]{0:T(128)}, u32[]{:S(2)}) copy-start(f32[128]{0:T(128)} %copy-done.53) | copy-start | bytes 1540
  768.3 423.5 %all-gather.24.cloned.1.call-start = ((), (), s32[]{:S(2)}) async-start(), calls=%async_computation.12 | async-start | bytes 8912896 | tf_op jit(solution)/shard_map/all_gather | solution.py:296
  769.4 515.4 %all-gather.26.cloned.1.call-start = ((), (), s32[]{:S(2)}) async-start(), calls=%async_computation.13 | async-start | bytes 8912896 | tf_op jit(solution)/shard_map/all_gather | solution.py:297
  1126.0 987.9 %reduce-scatter.8.cloned.1.call-start = ((), (), s32[]{:S(2)}) async-start(), calls=%async_computation.14 | async-start | bytes 71303168 | tf_op jit(solution)/shard_map/reduce_scatter | solution.py:322
  1478.7 1019.6 %all-reduce.4.cloned.1.call-start = ((), (), s32[]{:S(2)}) async-start(), calls=%async_computation.15 | async-start | bytes 33554432 | tf_op jit(solution)/shard_map/psum | solution.py:337
  (59 other events, 1230.4 us)
Sparse Core Ops, SparseCore 0:
  10.2 77.5 all-gather.15
  90.0 73.1 all-gather.9
  165.3 73.1 all-gather.13
  241.1 73.1 all-gather.17
  316.8 73.1 all-gather.11
  392.0 73.1 all-gather.19
  468.0 85.9 all-gather.21
  754.9 178.6 reduce-scatter.5
  937.7 177.5 reduce-scatter.3
  1117.9 73.9 all-gather.23
  1194.0 76.0 all-gather.25
  1478.8 635.0 reduce-scatter.7
  2117.1 381.0 all-reduce.3
